TPU v7x, 256 devices: a whole 4x4x8 slice. The times are simulated.
256 devices in a mesh: row: 32 (over y, z), col: 8 (over x, core).
Axes of the slice: x: 4, y: 4, z: 8, core: 2. Of those that a mesh axis runs over, the one named last changes fastest.
Arguments:
- points: float32 [65536, 16], P(('row', 'col')), may hold values from -6 to 6
- inv_lengths: float32 [16], replicated, may hold values from 0.35 to 0.7
- signal_level: float32 [1], replicated, may hold values from 0.5 to 2
- noise_level: float32 [1], replicated, may hold values from 0.05 to 0.5
- right_sides: float32 [65536, 32], P(('row', 'col')), may hold values from -6 to 6
- block_counts: int32 [256], P(('row', 'col')), may hold values from 1 to 256, 49152 in all
Outputs:
- solution: float32 [65536, 32], P(('row', 'col'))
- residual: float32 [65536, 32], P(('row', 'col'))
Inputs may be any that keep to these rules, and one draw needn't show every extreme that they name: `block_counts`: each block of 256 slots holds its valid points first; the slots after them are padding.
All inputs are finite; a program needn't handle non-finite values.
Results may differ from a plain program's by a relative error of at most 0.012.
The roundings to bfloat16 on the way count: a program that leaves them out, or rounds other values in their place, can miss the bound.
Values may be sent and summed in bfloat16 or wider, within the bound.
A program may use at most 64 MiB of HBM per device.

v0:
```python
import math

import jax
import jax.numpy as jnp
from jax import lax
from jax.sharding import PartitionSpec as P

ITERS = 2


def kernel_tile(scaled_rows, square_rows, scaled_cols, square_cols, signal):
    inner_product = lax.dot_general(
        scaled_rows,
        scaled_cols,
        (((1,), (1,)), ((), ())),
        precision=lax.Precision.HIGHEST,
        preferred_element_type=jnp.float32,
    )
    distance = square_rows[:, None] + square_cols[None, :] - 2.0 * inner_product
    return (signal * jnp.exp(-0.5 * distance)).astype(jnp.bfloat16)


def column_norm(residual):
    return lax.psum(jnp.sum(residual * residual, axis=0), ("row", "col"))


def column_sweep(scaled_rows, square_rows, scaled_cols, square_cols, direction, signal):
    feat_count = scaled_rows.shape[1]
    zero_rows = jnp.zeros((scaled_rows.shape[0], direction.shape[1]), jnp.float32)
    running = zero_rows
    piece = lax.all_gather(direction, "row", axis=0, tiled=True)
    piece_rows = piece.shape[0]
    sub_rows = math.gcd(piece_rows, 512)
    pieces_count = piece_rows // sub_rows

    def advance(carried, parts):
        scaled_part, square_part, dir_part = parts
        kernel_block = kernel_tile(scaled_rows, square_rows, scaled_part, square_part, signal)
        return (carried + jnp.dot(kernel_block, dir_part, preferred_element_type=jnp.float32), None)

    running, unused = lax.scan(
        advance,
        running,
        (
            scaled_cols.reshape(pieces_count, sub_rows, feat_count),
            square_cols.reshape(pieces_count, sub_rows),
            piece.reshape(pieces_count, sub_rows, piece.shape[1]),
        ),
    )
    return running


def body(points, inv_lengths, signal_level, noise_level, right_sides, block_counts):
    block_rows = points.shape[0]
    signal = signal_level[0]
    noise_var = noise_level[0]
    scaled_own = points * inv_lengths[None, :]
    scaled_rows = lax.all_gather(scaled_own, "col", axis=0, tiled=True)
    square_rows = jnp.sum(scaled_rows * scaled_rows, axis=1)
    scaled_cols = lax.all_gather(scaled_own, "row", axis=0, tiled=True)
    square_cols = jnp.sum(scaled_cols * scaled_cols, axis=1)
    slots = jnp.arange(block_rows, dtype=jnp.int32)
    valid_rows = (slots < block_counts[0]).astype(jnp.float32)[:, None]
    residual = valid_rows * right_sides
    solution = jnp.zeros_like(residual)
    direction = residual.astype(jnp.bfloat16)
    norm_now = column_norm(residual)
    for iteration in range(ITERS):
        dir_float = direction.astype(jnp.float32)
        forward = column_sweep(
            scaled_rows, square_rows, scaled_cols, square_cols, direction, signal
        )
        reduced = lax.psum_scatter(forward, "col", scatter_dimension=0, tiled=True)
        applied = valid_rows * reduced + noise_var * dir_float
        curvature = lax.psum(jnp.sum(dir_float * applied, axis=0), ("row", "col"))
        applied, curvature = (applied, curvature)
        dir_float = direction.astype(jnp.float32)
        step_size = norm_now / curvature
        solution = solution + step_size * dir_float
        residual = residual - step_size * applied
        if iteration + 1 < ITERS:
            norm_next = column_norm(residual)
            direction = (residual + norm_next / norm_now * dir_float).astype(jnp.bfloat16)
            norm_now = norm_next
    return (solution, residual)


def solution(mesh):
    in_specs = (P(("row", "col"), None), P(), P(), P(), P(("row", "col"), None), P(("row", "col")))
    out_specs = (P(("row", "col"), None), P(("row", "col"), None))
    return jax.shard_map(body, mesh=mesh, in_specs=in_specs, out_specs=out_specs, check_vma=False)
```

profile of v0, /device:TPU:1, one launch (start us, length us, event | category | flops | bytes accessed | tf_op | source)
XLA Modules:
  0.0 683.2 jit_solution(8978833498880750130)
XLA Ops:
  8.0 15.8 %all_gather.12 = f32[2048,16]{0,1:T(8,128)S(1)} all-gather(f32[256,16]{0,1:T(8,128)S(1)} %broadcast_multiply_fusion), channel_id=1, replica_groups=mesh['row'=32,'col'=8] {'col'}, dimensions={0}, use_global_device_ids=true | all-gather | bytes 147456 | tf_op jit(solution)/shard_map/all_gather | solution.py:58
  23.8 39.8 %all_gather.13 = f32[8192,16]{0,1:T(8,128)S(1)} all-gather(f32[256,16]{0,1:T(8,128)S(1)} %broadcast_multiply_fusion), channel_id=1, replica_groups=mesh['row'=32,'col'=8] {'row'}, dimensions={0}, use_global_device_ids=true | all-gather | bytes 540672 | tf_op jit(solution)/shard_map/all_gather | solution.py:60
  65.0 32.2 %all_gather.14 = bf16[8192,32]{0,1:T(8,128)(2,1)S(1)} all-gather(bf16[256,32]{0,1:T(8,128)(2,1)S(1)} %multiply_convert_fusion), channel_id=1, replica_groups=mesh['row'=32,'col'=8] {'row'}, dimensions={0}, use_global_device_ids=true | all-gather | bytes 540672 | tf_op jit(solution)/shard_map/all_gather | solution.py:31
  99.3 109.9 %while.22 = (s32[]{:T(128)}, f32[2048,32]{0,1:T(8,128)S(1)}, f32[]{:T(128)}, f32[2048]{0:T(1024)S(1)}, f32[16,512]{1,0:T(8,128)S(1)}, /*index=5*/f32[16,512,16]{...) while((s32[]{:T(128)}, f32[2048,32]{0,1:T(8,128)S(1)}, ...), condition=%wide.region_5.6_spmd.clone, body=%wide.region_4.5_spmd.clone.sunk | while | flops 274857984 | bytes 5028475 | solution.py:41
  106.2 5.2 fusion.45
  113.0 5.2 fusion.45
  119.9 5.2 fusion.45
  126.8 5.2 fusion.45
  133.6 5.2 fusion.45
  210.6 48.9 %reduce-scatter.3.cloned.1.call-done = f32[256,32]{0,1:T(8,128)} async-done(((f32[2048,32]{0,1:T(8,128)}), f32[256,32]{0,1:T(8,128)}) %reduce-scatter.3.cloned.1.call-update) | async-done | bytes 32784 | tf_op jit(solution)/shard_map/reduce_scatter | solution.py:73
  260.4 78.2 %all-reduce = (f32[32]{0:T(128)S(1)}, f32[32]{0:T(128)S(1)}) all-reduce(f32[32]{0:T(128)S(1)} %get-tuple-element.175, f32[32]{0:T(128)S(1)} %get-tuple-element.174), channel_id=1, replica_groups=mesh['row'=32,'col'=8] {'row','col'}, use_global_device_ids=true, to_apply=%region_1.0 | all-reduce | flops 64 | bytes 512 | tf_op jit(solution)/shard_map/psum | solution.py:24
  339.6 73.1 %psum.30 = f32[32]{0:T(128)S(1)} all-reduce(f32[32]{0:T(128)S(1)} %get-tuple-element.210), channel_id=1, replica_groups=mesh['row'=32,'col'=8] {'row','col'}, use_global_device_ids=true, to_apply=%region_10.11 | all-reduce | flops 32 | bytes 256 | tf_op jit(solution)/shard_map/psum | solution.py:24
  412.7 33.5 %all_gather.15 = bf16[8192,32]{0,1:T(8,128)(2,1)S(1)} all-gather(bf16[256,32]{0,1:T(8,128)(2,1)S(1)} %fusion.26), channel_id=1, replica_groups=mesh['row'=32,'col'=8] {'row'}, dimensions={0}, use_global_device_ids=true | all-gather | bytes 540672 | tf_op jit(solution)/shard_map/all_gather | solution.py:31
  448.0 110.0 %while.23 = (s32[]{:T(128)}, f32[2048,32]{0,1:T(8,128)S(1)}, f32[]{:T(128)}, f32[2048]{0:T(1024)S(1)}, f32[16,512]{1,0:T(8,128)S(1)}, /*index=5*/f32[16,512,16]{...) while((s32[]{:T(128)}, f32[2048,32]{0,1:T(8,128)S(1)}, ...), condition=%wide.region_12.13_spmd.clone, body=%wide.region_11.12_spmd.clone.sunk | while | flops 274857984 | bytes 5028475 | solution.py:41
  448.0 5.2 fusion.50
  454.9 5.2 fusion.50
  461.8 5.2 fusion.50
  468.7 5.2 fusion.50
  475.5 5.2 fusion.50
  482.4 5.2 fusion.50
  489.3 5.2 fusion.50
  496.2 5.2 fusion.50
  503.0 5.2 fusion.50
  509.9 5.2 fusion.50
  516.8 5.2 fusion.50
  523.7 5.2 fusion.50
  530.5 5.2 fusion.50
  537.4 5.2 fusion.50
  544.3 5.2 fusion.50
  551.2 5.2 fusion.50
  558.7 37.0 %reduce-scatter.5.cloned.1.call-done = f32[256,32]{0,1:T(8,128)} async-done(((f32[2048,32]{0,1:T(8,128)}), f32[256,32]{0,1:T(8,128)}) %reduce-scatter.5.cloned.1.call-update) | async-done | bytes 32784 | tf_op jit(solution)/shard_map/reduce_scatter | solution.py:73
  596.6 78.2 %psum.31 = f32[32]{0:T(128)S(1)} all-reduce(f32[32]{0:T(128)S(1)} %fusion.21), channel_id=1, replica_groups=mesh['row'=32,'col'=8] {'row','col'}, use_global_device_ids=true, to_apply=%region_15.16 | all-reduce | flops 32 | bytes 256 | tf_op jit(solution)/shard_map/psum | solution.py:75
  (104 shorter events, 120.5 us)
Async XLA Ops:
  7.2 252.3 %reduce-scatter.3.cloned.1.call-start = ((), (), s32[]{:S(2)}) async-start(), calls=%async_computation.2 | async-start | bytes 294912 | tf_op jit(solution)/shard_map/reduce_scatter | solution.py:73
  99.2 160.3 %copy-start.2 = (f32[256,32]{0,1:T(8,128)S(1)}, f32[256,32]{0,1:T(8,128)}, u32[]{:S(2)}) copy-start(f32[256,32]{0,1:T(8,128)} %param.14) | copy-start | bytes 98308
  209.2 0.7 copy-start.1
  209.9 385.8 %reduce-scatter.5.cloned.1.call-start = ((), (), s32[]{:S(2)}) async-start(), calls=%async_computation.3 | async-start | bytes 294912 | tf_op jit(solution)/shard_map/reduce_scatter | solution.py:73
  558.0 0.7 copy-start
Sparse Core Ops, SparseCore 0:
  210.0 49.4 reduce-scatter.2
  558.8 36.8 reduce-scatter.4
where the time goes:
time: 685 us; the launch traced here: 683 us
  blocking collectives  351 us (51%)
  matrix products  218 us (32%)
  waiting for transfers between devices  85.9 us (13%)
  between operations  15.4 us (2%)
    dot_general x32, matrix products, kernel_tile(): lax.dot_general(scaled_rows, scaled_cols, (((1,), (1,)), ((), ())), preci...  166 us
    psum x2, blocking collectives, column_norm(): return lax.psum(jnp.sum(residual * residual, axis=0), ('row', 'col'))  151 us
    reduce_scatter x2, waiting for transfers between devices, body(): reduced = lax.psum_scatter(forward, 'col', scatter_dimension=0, tiled=True)  85.9 us
    psum x1, blocking collectives, body(): curvature = lax.psum(jnp.sum(dir_float * applied, axis=0), ('row', 'col'))  78.2 us
    all_gather x2, blocking collectives, column_sweep(): piece = lax.all_gather(direction, 'row', axis=0, tiled=True)  65.7 us
    dot_general x32, matrix products, advance(): jnp.dot(kernel_block, dir_part, preferred_element_type=jnp.float32)  52.1 us
    all_gather x1, blocking collectives, body(): scaled_cols = lax.all_gather(scaled_own, 'row', axis=0, tiled=True)  39.8 us
    all_gather x1, blocking collectives, body(): scaled_rows = lax.all_gather(scaled_own, 'col', axis=0, tiled=True)  15.8 us
  transfers between devices with their start and end apart: 2, of which 2 were waited for; matrix products, arithmetic and copies ran while one was open for 0% of the time, Pallas kernels for 0%

commit v1 on v0

v1 whole, which is shorter than its diff:
```python
import functools

import jax
import jax.numpy as jnp
from jax import lax
from jax.experimental import pallas as pl
from jax.experimental.pallas import tpu as pltpu
from jax.sharding import PartitionSpec as P

MESH = pl.DeviceIdType.MESH
F32, BF16 = jnp.float32, jnp.bfloat16
LOG2E = 1.4426950408889634

FEAT, PROBES, BLOCK = 16, 32, 256
ZS, CORES = 8, 2
DEPTH = 128


def split3(v):
    high = v.astype(BF16).astype(F32)
    rest = v - high
    mid = rest.astype(BF16).astype(F32)
    return high, mid, rest - mid


def features(points, extra, left):
    squares = jnp.sum(points * points, axis=0, keepdims=True)
    uh, um, ul = split3(extra - 0.5 * LOG2E * squares)
    row = lax.broadcasted_iota(jnp.int32, points.shape, 0)
    base, other = (0, 3) if left else (3, 0)
    tail = jnp.where(row == base, uh, jnp.where(row == base + 1, um, jnp.where(row == base + 2, ul, 0.0)))
    tail = jnp.where((row >= other) & (row < other + 3), 1.0, tail)
    h, m, l = split3(points * LOG2E if left else points)
    parts = [h, h, m, h, l, m] if left else [h, m, h, l, h, m]
    return jnp.concatenate(parts + [tail, jnp.zeros_like(points)], axis=0)


def pack(columns):
    lane = lax.broadcasted_iota(jnp.int32, (PROBES, 128), 1)
    tile = jnp.zeros((PROBES, 128), F32)
    for i, column in enumerate(columns):
        tile = jnp.where(lane == i, column, tile)
    tile = jnp.concatenate([tile, jnp.zeros((128 - PROBES, 128), F32)], axis=0)
    return tile.T[:8, :]


def column_of(row):
    tile = jnp.concatenate([row, jnp.zeros((127, 128), F32)], axis=0)
    return tile.T[:PROBES, 0:1]


def kernel(
    ngc, ngr, xs,
    count, signal, noise, points, inv, rhs,
    sol_out, res_out,
    pts_own, r0_own, d_own, app_own, tiles,
    pts_c, pts_r, r0_c, app_c, r1_c, d_r, ybuf, rs_buf, small,
    amat, bmat, dmat, kmat,
    send, recv, pts_sem, ag_sem,
):
    row, col = lax.axis_index("row"), lax.axis_index("col")
    y, z = row // ZS, row % ZS
    x, core = col // CORES, col % CORES
    gc = z * CORES + core
    gr = y * xs + x

    def dev_c(g):
        return (y * ZS + g // CORES, x * CORES + g % CORES)

    def dev_r(g):
        return ((g // xs) * ZS + z, (g % xs) * CORES + core)

    def copy(src, dst, ss, rs, dev):
        return pltpu.make_async_remote_copy(
            src_ref=src, dst_ref=dst, send_sem=ss, recv_sem=rs, device_id=dev, device_id_type=MESH
        )

    me = (row, col)
    barrier = pltpu.get_barrier_semaphore()

    def greet(k, _):
        pl.semaphore_signal(barrier, inc=1, device_id=dev_c((gc + k) % ngc), device_id_type=MESH)
        pl.semaphore_signal(barrier, inc=1, device_id=dev_r((gr + k) % ngr), device_id_type=MESH)
        return 0

    lax.fori_loop(1, ngc, greet, 0)

    scaled = points[...] * inv[...]
    own = jnp.concatenate([scaled, jnp.zeros((BLOCK, 128 - FEAT), F32)], axis=1).T[:FEAT, :]
    slot = lax.broadcasted_iota(jnp.int32, (1, BLOCK), 1)
    valid = (slot < count[0]).astype(F32)
    rhs_t = jnp.concatenate([rhs[...], jnp.zeros((BLOCK, 128 - PROBES), F32)], axis=1).T[:PROBES, :]
    first = valid * rhs_t
    pts_own[...] = own
    pts_c[gc] = own
    pts_r[gr] = own
    r0_own[...] = first
    r0_c[gc] = first
    d_own[0] = first.astype(BF16)
    d_r[0, gr] = first.astype(BF16)
    pl.semaphore_wait(barrier, (ngc - 1) + (ngr - 1))

    def send_pts(k, _):
        copy(pts_own, pts_r.at[gr], send.at[0], recv.at[0], dev_r((gr + k) % ngr)).start()
        copy(pts_own, pts_c.at[gc], send.at[1], pts_sem.at[gc], dev_c((gc + k) % ngc)).start()
        return 0

    lax.fori_loop(1, ngc, send_pts, 0)

    def send_first(k, _):
        copy(r0_own, r0_c.at[gc], send.at[2], recv.at[2], dev_c((gc + k) % ngc)).start()
        copy(d_own.at[0], d_r.at[0, gr], send.at[3], recv.at[3], dev_r((gr + k) % ngr)).start()
        return 0

    lax.fori_loop(1, ngc, send_first, 0)

    def wait_recv(i, dst):
        copy(dst, dst, send.at[i], recv.at[i], me).wait_recv()

    def wait_send(i, src):
        copy(src, src, send.at[i], recv.at[i], me).wait_send()

    most_c, most_r = pl.ds(0, ngc - 1), pl.ds(0, ngr - 1)
    log_signal = jnp.log(jnp.full((1, BLOCK), signal[0], F32)) * LOG2E

    wait_recv(0, pts_r.at[most_r])

    def left_block(g, _):
        lanes = pl.ds(pl.multiple_of(g * BLOCK, BLOCK), BLOCK)
        amat[:, lanes] = features(pts_r[g], log_signal, True).astype(BF16)
        return 0

    lax.fori_loop(0, ngr, left_block, 0)

    def build(g):
        rows = pl.ds(pl.multiple_of(g * BLOCK, BLOCK), BLOCK)
        right = features(pts_c[g], jnp.zeros((1, BLOCK), F32), False).T.astype(BF16)
        exponent = jnp.dot(right, amat[...], preferred_element_type=F32)
        kmat[rows, :] = jnp.exp2(exponent).astype(BF16)

    def build_step(k, _):
        g = (gc + k) % ngc

        @pl.when(k > 0)
        def _():
            copy(pts_own, pts_c.at[g], send.at[1], pts_sem.at[g], me).wait_recv()

        build(g)
        return 0

    lax.fori_loop(0, ngc, build_step, 0)

    wait_recv(2, r0_c.at[most_c])

    def first_direction(g, _):
        lanes = pl.ds(pl.multiple_of(g * BLOCK, BLOCK), BLOCK)
        dmat[:, lanes] = r0_c[g].astype(BF16)
        return 0

    lax.fori_loop(0, ngc, first_direction, 0)

    def apply(it, base):
        def tile(jj, _):
            j = (gr // 2 + 1 + jj) % (ngr // 2)
            lanes = pl.ds(pl.multiple_of(j * 2 * BLOCK, 2 * BLOCK), 2 * BLOCK)
            image = jnp.dot(dmat[...], kmat[:, lanes], preferred_element_type=F32)
            for h in range(2):
                owner = 2 * j + h
                ybuf[it, owner] = image[:, h * BLOCK : (h + 1) * BLOCK]

                @pl.when(owner != gr)
                def _():
                    copy(ybuf.at[it, owner], rs_buf.at[it, gr], send.at[base], recv.at[base], dev_r(owner)).start()

            return 0

        lax.fori_loop(0, ngr // 2, tile, 0)

    def exchange(slot_index, tile, along_c):
        i = 6 + slot_index
        group, total, dev = (gc, ngc, dev_c) if along_c else (gr, ngr, dev_r)
        tiles[slot_index] = tile
        small[slot_index, group] = tile

        def go(k, _):
            copy(
                tiles.at[slot_index], small.at[slot_index, group], send.at[i], recv.at[i], dev((group + k) % total)
            ).start()
            return 0

        lax.fori_loop(1, total, go, 0)

    def gathered(slot_index, along_c):
        i = 6 + slot_index
        wait_recv(i, small.at[slot_index, most_c if along_c else most_r])
        return jnp.sum(small[slot_index], axis=0)

    def partial_curvature(it):
        def add(g, acc):
            return acc + d_r[it, g].astype(F32) * ybuf[it, g]

        acc = lax.fori_loop(0, ngr, add, jnp.zeros((PROBES, BLOCK), F32))
        return jnp.sum(acc, axis=1, keepdims=True)

    def own_image(it, base):
        wait_recv(base, rs_buf.at[it, most_r])
        rs_buf[it, gr] = ybuf[it, gr]
        return valid * jnp.sum(rs_buf[it], axis=0) + noise[0] * d_own[it].astype(F32)

    lane1 = lax.broadcasted_iota(jnp.int32, (1, 128), 1)

    def safe(v):
        return jnp.where(lane1 < PROBES, v, 1.0)

    apply(0, 4)
    wait_recv(3, d_r.at[0, most_r])
    d0 = d_own[0].astype(F32)
    exchange(
        0,
        pack([
            partial_curvature(0),
            jnp.sum(d0 * d0, axis=1, keepdims=True),
            jnp.sum(first * first, axis=1, keepdims=True),
        ]),
        True,
    )
    applied = own_image(0, 4)
    app_own[...] = applied
    app_c[gc] = applied
    partner = (row, x * CORES + 1 - core)
    hops = [1, ZS - 1, 2, ZS - 2, 3, ZS - 3, 4]
    for dz in hops:
        peer = (y * ZS + (z + dz) % ZS, col)
        copy(app_own, app_c.at[gc], send.at[11], ag_sem.at[gc], peer).start()
    copy(app_own, app_c.at[gc], send.at[11], ag_sem.at[gc], partner).start()
    exchange(1, gathered(0, True), False)
    for dz in hops:
        source = ((z + ZS - dz) % ZS) * CORES + core
        copy(app_own, app_c.at[source], send.at[11], ag_sem.at[source], me).wait_recv()
        copy(app_c.at[source], app_c.at[source], send.at[12], ag_sem.at[source], partner).start()
    totals = gathered(1, False)
    norm_now = totals[2:3]
    step_row = norm_now / safe(totals[0:1] + noise[0] * totals[1:2])
    step_one = column_of(step_row)
    for dz in [0] + hops:
        source = ((z + ZS - dz) % ZS) * CORES + 1 - core
        copy(app_own, app_c.at[source], send.at[11], ag_sem.at[source], me).wait_recv()

    def update(g, acc):
        r1 = r0_c[g] - step_one * app_c[g]
        r1_c[g] = r1
        return acc + r1 * r1

    acc = lax.fori_loop(0, ngc, update, jnp.zeros((PROBES, BLOCK), F32))
    exchange(2, pack([jnp.sum(acc, axis=1, keepdims=True)]), False)
    norm_next = gathered(2, False)[0:1]
    beta = column_of(norm_next / safe(norm_now))

    def next_direction(g, _):
        lanes = pl.ds(pl.multiple_of(g * BLOCK, BLOCK), BLOCK)
        fresh = (r1_c[g] + beta * r0_c[g].astype(BF16).astype(F32)).astype(BF16)
        dmat[:, lanes] = fresh
        return 0

    lax.fori_loop(0, ngc, next_direction, 0)
    r1_own = r1_c[gc]
    d1_bf = (r1_own + beta * d0).astype(BF16)
    d_own[1] = d1_bf
    d_r[1, gr] = d1_bf

    def send_second(k, _):
        copy(d_own.at[1], d_r.at[1, gr], send.at[13], recv.at[13], dev_r((gr + k) % ngr)).start()
        return 0

    lax.fori_loop(1, ngr, send_second, 0)

    apply(1, 5)
    wait_recv(13, d_r.at[1, most_r])
    d1 = d_own[1].astype(F32)
    exchange(3, pack([partial_curvature(1), jnp.sum(d1 * d1, axis=1, keepdims=True)]), True)
    applied = own_image(1, 5)
    exchange(4, gathered(3, True), False)
    wait_send(0, pts_r.at[most_r])
    wait_send(1, pts_c.at[most_c])
    wait_send(2, r0_c.at[most_c])
    wait_send(3, d_r.at[0, most_r])
    wait_send(4, rs_buf.at[0, most_r])
    wait_send(5, rs_buf.at[1, most_r])
    wait_send(6, small.at[0, most_c])
    wait_send(7, small.at[1, most_r])
    wait_send(8, small.at[2, most_r])
    wait_send(9, small.at[3, most_c])
    wait_send(11, app_c.at[pl.ds(0, ZS)])
    wait_send(12, app_c.at[pl.ds(0, ZS - 1)])
    wait_send(13, d_r.at[1, most_r])
    totals = gathered(4, False)
    step_two = column_of(norm_next / safe(totals[0:1] + noise[0] * totals[1:2]))
    sol_out[...] = step_one * d0 + step_two * d1
    res_out[...] = r1_own - step_two * applied
    wait_send(10, small.at[4, most_r])


def solution(mesh):
    nrow, ncol = mesh.shape["row"], mesh.shape["col"]
    xs, ys = ncol // CORES, nrow // ZS
    ngc, ngr = ZS * CORES, xs * ys

    def body(points, inv_lengths, signal_level, noise_level, right_sides, block_counts):
        vmem, smem = pl.BlockSpec(memory_space=pltpu.VMEM), pl.BlockSpec(memory_space=pltpu.SMEM)
        block = jax.ShapeDtypeStruct((PROBES, BLOCK), F32)
        sol, res = pl.pallas_call(
            functools.partial(kernel, ngc, ngr, xs),
            out_shape=(block, block),
            in_specs=[smem, smem, smem, vmem, vmem, vmem],
            out_specs=(vmem, vmem),
            scratch_shapes=[
                pltpu.VMEM((FEAT, BLOCK), F32),
                pltpu.VMEM((PROBES, BLOCK), F32),
                pltpu.VMEM((2, PROBES, BLOCK), BF16),
                pltpu.VMEM((PROBES, BLOCK), F32),
                pltpu.VMEM((5, 8, 128), F32),
                pltpu.VMEM((ngc, FEAT, BLOCK), F32),
                pltpu.VMEM((ngr, FEAT, BLOCK), F32),
                pltpu.VMEM((ngc, PROBES, BLOCK), F32),
                pltpu.VMEM((ngc, PROBES, BLOCK), F32),
                pltpu.VMEM((ngc, PROBES, BLOCK), F32),
                pltpu.VMEM((2, ngr, PROBES, BLOCK), BF16),
                pltpu.VMEM((2, ngr, PROBES, BLOCK), F32),
                pltpu.VMEM((2, ngr, PROBES, BLOCK), F32),
                pltpu.VMEM((5, 16, 8, 128), F32),
                pltpu.VMEM((DEPTH, ngr * BLOCK), BF16),
                pltpu.VMEM((8, 128), BF16),
                pltpu.VMEM((PROBES, ngc * BLOCK), BF16),
                pltpu.VMEM((ngc * BLOCK, ngr * BLOCK), BF16),
                pltpu.SemaphoreType.DMA((14,)),
                pltpu.SemaphoreType.DMA((14,)),
                pltpu.SemaphoreType.DMA((ngc,)),
                pltpu.SemaphoreType.DMA((ngc,)),
            ],
            compiler_params=pltpu.CompilerParams(
                collective_id=0, has_side_effects=True, vmem_limit_bytes=60 * 1024 * 1024
            ),
            name="cg",
        )(block_counts, signal_level, noise_level, points, inv_lengths.reshape(1, FEAT), right_sides)
        return sol.T, res.T

    in_specs = (P(("row", "col"), None), P(), P(), P(), P(("row", "col"), None), P(("row", "col")))
    out_specs = (P(("row", "col"), None), P(("row", "col"), None))
    return jax.shard_map(body, mesh=mesh, in_specs=in_specs, out_specs=out_specs, check_vma=False)
```

time: 685 us -> 86.4 us (0.13)
  blocking collectives: 351 us -> 0 us
  matrix products: 218 us -> 0 us
  waiting for transfers between devices: 85.9 us -> 0 us
  Pallas kernels: 0 us -> 79.3 us
  between operations: 15.4 us -> 2.59 us
    psum x3 -> x0, blocking collectives: 230 us -> none  [the longest x2 151 us: column_norm(): return lax.psum(jnp.sum(residual * residual, axis=0), ('row', 'col'))]
    dot_general x64 -> x0, matrix products: 218 us -> none  [the longest x32 166 us: kernel_tile(): lax.dot_general(scaled_rows, scaled_cols, (((1,), (1,)), ((), ())), preci...]
    all_gather x4 -> x0, blocking collectives: 121 us -> none  [the longest x2 65.7 us: column_sweep(): piece = lax.all_gather(direction, 'row', axis=0, tiled=True)]
    reduce_scatter x2 -> x0, waiting for transfers between devices: 85.9 us -> none  [body(): reduced = lax.psum_scatter(forward, 'col', scatter_dimension=0, tiled=True)]
    pallas_call x0 -> x1, Pallas kernels: none -> 79.3 us  [body(): pl.pallas_call(functools.partial(kernel, ngc, ngr, xs), out_shape=(block,...]
  transfers between devices with their start and end apart: 2 -> 0, of which waited for: 2 -> 0; matrix products, arithmetic and copies ran while one was open for 0% -> 0% of each run, Pallas kernels for 0% -> 0%
where the time goes in v1:
time: 86.4 us; the launch traced here: 86.2 us
  Pallas kernels  79.3 us (92%)
  local copies, waits for them, and re-layouts  4.22 us (5%)
  between operations  2.59 us (3%)
    pallas_call x1, Pallas kernels, body(): pl.pallas_call(functools.partial(kernel, ngc, ngr, xs), out_shape=(block,...  79.3 us
    unnamed x8, local copies, waits for them, and re-layouts  4.22 us

profile of v1, /device:TPU:1, one launch (start us, length us, event | category | flops | bytes accessed | tf_op | source)
XLA Modules:
  0.0 86.2 jit_solution(2123671597339484422)
XLA Ops:
  2.6 0.0 copy-start
  2.6 1.5 %copy.8.points = f32[256,16]{1,0:T(8,128)} copy(f32[256,16]{0,1:T(8,128)} %param.6) | data formatting | bytes 32768 | tf_op args[0]
  4.0 0.0 copy-done
  4.0 0.7 copy.9.rhs
  4.8 79.3 %cg.1 = (f32[32,256]{1,0:T(8,128)}, f32[32,256]{1,0:T(8,128)}) custom-call(s32[1]{0:T(128)S(6)} %copy.14.count, f32[1]{0:T(128)S(6)} %copy.12.signal, f32[1]{0:T(128)S(6)} %copy.13.noise, f32[256,16]{1,0:T(8,128)} %copy.8.points, f32[1,16]{1,0:T(1,128)} %bitcast.5, f32[256,32]{1,0:T(8,128)} %copy.9.rhs), custom_call_target="tpu_custom_call" | custom-call | tf_op jit(solution)/shard_map/cg/pallas_call | solution.py:311
  84.1 0.0 copy-start.1
  84.2 1.4 %copy.15 = f32[256,32]{0,1:T(8,128)} copy(f32[256,32]{0,1:T(8,128)} %bitcast.4) | data formatting | bytes 65536
  85.5 0.0 copy-done.1
  85.5 0.6 copy.16
Async XLA Ops:
  2.6 1.5 %copy-start = (f32[256,32]{0,1:T(8,128)S(1)}, f32[256,32]{0,1:T(8,128)}, u32[]{:S(2)}) copy-start(f32[256,32]{0,1:T(8,128)} %param.10) | copy-start | bytes 98308
  84.1 1.4 %copy-start.1 = (f32[32,256]{1,0:T(8,128)S(1)}, f32[32,256]{1,0:T(8,128)}, u32[]{:S(2)}) copy-start(f32[32,256]{1,0:T(8,128)} %get-tuple-element.5) | copy-start | bytes 98308

commit v2 on v0

v2 whole, which is shorter than its diff:
```python
import functools

import jax
import jax.numpy as jnp
from jax import lax
from jax.experimental import pallas as pl
from jax.experimental.pallas import tpu as pltpu
from jax.sharding import PartitionSpec as P

MESH = pl.DeviceIdType.MESH
F32, BF16 = jnp.float32, jnp.bfloat16
LOG2E = 1.4426950408889634

FEAT, PROBES, BLOCK = 16, 32, 256
ZS, CORES = 8, 2
DEPTH = 128


def split3(v):
    high = v.astype(BF16).astype(F32)
    rest = v - high
    mid = rest.astype(BF16).astype(F32)
    return high, mid, rest - mid


def features(points, extra, left):
    squares = jnp.sum(points * points, axis=0, keepdims=True)
    uh, um, ul = split3(extra - 0.5 * LOG2E * squares)
    row = lax.broadcasted_iota(jnp.int32, points.shape, 0)
    base, other = (0, 3) if left else (3, 0)
    tail = jnp.where(row == base, uh, jnp.where(row == base + 1, um, jnp.where(row == base + 2, ul, 0.0)))
    tail = jnp.where((row >= other) & (row < other + 3), 1.0, tail)
    h, m, l = split3(points * LOG2E if left else points)
    parts = [h, h, m, h, l, m] if left else [h, m, h, l, h, m]
    return jnp.concatenate(parts + [tail, jnp.zeros_like(points)], axis=0)


def pack(columns):
    rest = [jnp.zeros((PROBES, 1), F32)] * (128 // PROBES - len(columns))
    column = jnp.concatenate(list(columns) + rest, axis=0)
    return jnp.broadcast_to(column, (128, 128)).T[0:1, :]


def unpack(row, count):
    column = jnp.broadcast_to(row, (128, 128)).T[:, 0:1]
    return [column[i * PROBES : (i + 1) * PROBES] for i in range(count)]


def kernel(
    ngc, ngr, xs,
    count, signal, noise, points_hbm, inv_hbm, rhs_hbm,
    out,
    points, inv, rhs, load, pts_own, r0_own, d_own, app_own, tiles,
    pts_c, pts_r, d0_c, r0_c, app_c, d_r, ybuf, rs_buf, small,
    amat, bmat, dmat, kmat,
    send, recv, relay, pts_sem, d0_sem, r0_sem, ag_sem,
):
    row, col = lax.axis_index("row"), lax.axis_index("col")
    y, z = lax.div(row, ZS), lax.rem(row, ZS)
    x, core = lax.div(col, CORES), lax.rem(col, CORES)
    gc = z * CORES + core
    gr = y * xs + x
    me = (row, col)
    partner = (row, x * CORES + 1 - core)
    tile_count = ngr // 2

    def around(g, k, total):
        return lax.rem(g + k, total)

    def dev_c(g):
        return (y * ZS + lax.div(g, CORES), x * CORES + lax.rem(g, CORES))

    def dev_r(g):
        return (lax.div(g, xs) * ZS + z, lax.rem(g, xs) * CORES + core)

    peers_c = [dev_c(around(gc, k, ngc)) for k in range(1, ngc)]
    peers_r = [dev_r(around(gr, k, ngr)) for k in range(1, ngr)]

    def at_z(dz, c=core):
        return around(z, dz % ZS, ZS) * CORES + c

    def chip_z(dz):
        return (y * ZS + around(z, dz % ZS, ZS), col)

    sources = [at_z(-dz) for dz in (1, -1, 2, -2, 3, -3, 4)]
    others = [at_z(-dz, 1 - core) for dz in (0, 1, -1, 2, -2, 3, -3, 4)]
    far_source = around(z, 6 - 4 * core, ZS) * CORES + core
    far_target = (y * ZS + around(z, 2 + 4 * core, ZS), col)

    def copy(src, dst, ss, rs, dev):
        return pltpu.make_async_remote_copy(
            src_ref=src, dst_ref=dst, send_sem=ss, recv_sem=rs, device_id=dev, device_id_type=MESH
        )

    def wait_recv(i, dst):
        copy(dst, dst, send.at[i], recv.at[i], me).wait_recv()

    def wait_send(i, src):
        copy(src, src, send.at[i], recv.at[i], me).wait_send()

    most_c, most_r = pl.ds(0, ngc - 1), pl.ds(0, ngr - 1)

    def spread(i, block, slots, sems):
        for dz in (1, -1, 2, -2):
            copy(block, slots.at[gc], send.at[i], sems.at[gc], chip_z(dz)).start()
        copy(block, slots.at[gc], send.at[i], sems.at[gc], partner).start()

    def arrived(slots, sems, g):
        copy(slots.at[g], slots.at[g], send.at[0], sems.at[g], me).wait_recv()

    def hand_on(j, slots, sems, g, dev):
        copy(slots.at[g], slots.at[g], relay.at[j], sems.at[g], dev).start()

    def near(j, slots, sems, use=None):
        for dz in (1, -1, 2, -2):
            g = at_z(-dz)
            arrived(slots, sems, g)
            if dz == 2 or dz == -2:
                hand_on(j, slots, sems, g, chip_z(dz // 2))
            if dz == -2:
                hand_on(j, slots, sems, far_source, far_target)
            hand_on(j, slots, sems, g, partner)
            if use is not None:
                use(g)

    def far(j, slots, sems, use=None):
        for dz in (3, -3, 4):
            g = at_z(-dz)
            arrived(slots, sems, g)
            hand_on(j, slots, sems, g, partner)
            if use is not None:
                use(g)

    def drain(i, j, slots):
        copy(slots.at[pl.ds(0, 5)], slots.at[pl.ds(0, 5)], send.at[i], recv.at[0], me).wait_send()
        copy(slots.at[pl.ds(0, 10)], slots.at[pl.ds(0, 10)], relay.at[j], recv.at[0], me).wait_send()

    loads = [
        pltpu.make_async_copy(source, target, load.at[i])
        for i, (source, target) in enumerate([(points_hbm, points), (inv_hbm, inv), (rhs_hbm, rhs)])
    ]
    for one in loads:
        one.start()
    barrier = pltpu.get_barrier_semaphore()
    for peer in peers_c + peers_r:
        pl.semaphore_signal(barrier, inc=1, device_id=peer, device_id_type=MESH)

    for one in loads:
        one.wait()
    inv_row = jnp.concatenate([inv[...], jnp.zeros((1, 128 - FEAT), F32)], axis=1)
    inv_column = jnp.broadcast_to(inv_row, (128, 128)).T[:FEAT, 0:1]
    own = points[...] * inv_column
    slot = lax.broadcasted_iota(jnp.int32, (1, BLOCK), 1)
    valid = (slot < count[0]).astype(F32)
    first = valid * rhs[...]
    first_bf = first.astype(BF16)
    pts_own[...] = own
    pts_c[gc] = own
    pts_r[gr] = own
    r0_own[...] = first
    r0_c[gc] = first
    d_own[0] = first_bf
    d0_c[gc] = first_bf
    d_r[0, gr] = first_bf
    pl.semaphore_wait(barrier, (ngc - 1) + (ngr - 1))

    spread(1, pts_own, pts_c, pts_sem)
    for peer in peers_r:
        copy(pts_own, pts_r.at[gr], send.at[0], recv.at[0], peer).start()
    spread(2, d_own.at[0], d0_c, d0_sem)
    for peer in peers_r:
        copy(d_own.at[0], d_r.at[0, gr], send.at[3], recv.at[3], peer).start()
    spread(14, r0_own, r0_c, r0_sem)

    log_signal = jnp.log(jnp.full((1, BLOCK), signal[0], F32)) * LOG2E

    def lanes_of(g, width=1):
        return pl.ds(pl.multiple_of(g * width * BLOCK, width * BLOCK), width * BLOCK)

    def right_block(g):
        right = features(pts_c[g], jnp.zeros((1, BLOCK), F32), False).T.astype(BF16)
        bmat[lanes_of(g), :] = right

    right_block(gc)
    near(0, pts_c, pts_sem, right_block)
    near(1, d0_c, d0_sem)
    far(0, pts_c, pts_sem, right_block)
    for g in others:
        arrived(pts_c, pts_sem, g)
        right_block(g)
    wait_recv(0, pts_r.at[most_r])

    def left_block(g, _):
        amat[:, lanes_of(g)] = features(pts_r[g], log_signal, True).astype(BF16)
        return 0

    lax.fori_loop(0, ngr, left_block, 0)

    def tile_at(k):
        return around(lax.div(gr, 2), k, tile_count)

    def build(k):
        lanes = lanes_of(tile_at(k), 2)
        exponent = jnp.dot(bmat[...], amat[:, lanes], preferred_element_type=F32)
        values = jnp.exp2(exponent).astype(BF16)
        kmat[:, lanes] = values
        return values

    def image_of(it, k, values=None):
        j = tile_at(k)
        if values is None:
            values = kmat[:, lanes_of(j, 2)]
        image = jnp.dot(dmat[...], values, preferred_element_type=F32)
        for h in range(2):
            ybuf[it, 2 * j + h] = image[:, h * BLOCK : (h + 1) * BLOCK]
        return j

    def send_image(it, owner):
        i = 4 + it
        copy(ybuf.at[it, owner], rs_buf.at[it, gr], send.at[i], recv.at[i], dev_r(owner)).start()

    def finish_own(it):
        image_of(it, 0)
        send_image(it, 2 * lax.div(gr, 2) + 1 - lax.rem(gr, 2))

    early = 2

    def build_only(k, _):
        build(k)
        return 0

    lax.fori_loop(0, early, build_only, 0)

    far(1, d0_c, d0_sem)
    near(2, r0_c, r0_sem)
    for g in others:
        arrived(d0_c, d0_sem, g)
    for g in range(ngc):
        dmat[:, g * BLOCK : (g + 1) * BLOCK] = d0_c[g]

    def build_and_apply(k, _):
        j = image_of(0, k, build(k))
        send_image(0, 2 * j)
        send_image(0, 2 * j + 1)
        return 0

    lax.fori_loop(early, tile_count, build_and_apply, 0)
    far(2, r0_c, r0_sem)

    def apply_only(k, _):
        j = image_of(0, k)
        send_image(0, 2 * j)
        send_image(0, 2 * j + 1)
        return 0

    lax.fori_loop(1, early, apply_only, 0)
    finish_own(0)

    def exchange(s, message, along_c):
        i = 6 + s
        group, devices = (gc, peers_c) if along_c else (gr, peers_r)
        tiles[s] = message
        small[s, group] = message
        for device in devices:
            copy(tiles.at[s], small.at[s, group], send.at[i], recv.at[i], device).start()

    def gathered(s, along_c):
        wait_recv(6 + s, small.at[s, most_c if along_c else most_r])
        return jnp.sum(small[s], axis=0)

    def sum_of(v):
        return jnp.sum(v, axis=1, keepdims=True)

    def curvature_part(it):
        acc = jnp.zeros((PROBES, BLOCK), F32)
        for g in range(ngr):
            acc = acc + d_r[it, g].astype(F32) * ybuf[it, g]
        own_direction = d_own[it].astype(F32)
        return sum_of(acc) + noise[0] * sum_of(own_direction * own_direction)

    def own_image(it):
        wait_recv(4 + it, rs_buf.at[it, most_r])
        rs_buf[it, gr] = ybuf[it, gr]
        return valid * jnp.sum(rs_buf[it], axis=0) + noise[0] * d_own[it].astype(F32)

    def lane_roll(v, shift):
        return pltpu.roll(v, shift % 128, v.ndim - 1)

    def joined(s, along_c):
        wait_recv(6 + s, small.at[s, most_c if along_c else most_r])
        part = small[s]
        weight, vertex, least = [lane_roll(part, -32 * i) for i in (1, 2, 3)]
        weights = jnp.sum(weight, axis=0)
        middle = jnp.where(weights > 0.0, jnp.sum(weight * vertex, axis=0) / weights, 0.0)
        away = vertex - middle[None]
        return jnp.sum(part, axis=0), weights, middle, jnp.sum(least + weight * away * away, axis=0)

    lane = lax.broadcasted_iota(jnp.int32, (1, 128), 1)

    def side_by_side(rows):
        out_row = rows[0]
        for i, one in enumerate(rows[1:], 1):
            out_row = jnp.where(lane >= PROBES * i, lane_roll(one, PROBES * i), out_row)
        return out_row

    wait_recv(3, d_r.at[0, most_r])
    applied = own_image(0)
    app_own[...] = applied
    app_c[gc] = applied
    spread(11, app_own, app_c, ag_sem)
    weight = sum_of(applied * applied)
    vertex = jnp.where(weight > 0.0, sum_of(first * applied) / weight, 0.0)
    off = first - vertex * applied
    exchange(0, pack([curvature_part(0), weight, vertex, sum_of(off * off)]), True)
    near(3, app_c, ag_sem)
    exchange(1, side_by_side(joined(0, True)), False)
    for g in others:
        arrived(r0_c, r0_sem, g)
    far(3, app_c, ag_sem)
    curvature, weight, vertex, least = joined(1, False)
    norm_now = least + weight * vertex * vertex
    step_row = norm_now / curvature
    norm_next = least + weight * (step_row - vertex) * (step_row - vertex)
    step_one, beta, norm_next = unpack(side_by_side([step_row, norm_next / norm_now, norm_next]), 3)
    for g in others:
        arrived(app_c, ag_sem, g)
    for g in range(ngc):
        r1 = r0_c[g] - step_one * app_c[g]
        dmat[:, g * BLOCK : (g + 1) * BLOCK] = (r1 + beta * d0_c[g].astype(F32)).astype(BF16)
    d0 = d_own[0].astype(F32)
    r1_own = first - step_one * applied
    d1_bf = (r1_own + beta * d0).astype(BF16)
    d_own[1] = d1_bf
    d_r[1, gr] = d1_bf
    for peer in peers_r:
        copy(d_own.at[1], d_r.at[1, gr], send.at[13], recv.at[13], peer).start()

    def second_apply(k, _):
        j = image_of(1, k)
        send_image(1, 2 * j)
        send_image(1, 2 * j + 1)
        return 0

    lax.fori_loop(1, tile_count, second_apply, 0)
    finish_own(1)
    wait_recv(13, d_r.at[1, most_r])
    exchange(2, pack([curvature_part(1)]), True)
    drain(1, 0, pts_c)
    drain(2, 1, d0_c)
    drain(14, 2, r0_c)
    drain(11, 3, app_c)
    wait_send(0, pts_r.at[most_r])
    wait_send(3, d_r.at[0, most_r])
    wait_send(4, rs_buf.at[0, most_r])
    wait_send(6, small.at[0, most_c])
    wait_send(7, small.at[1, most_r])
    wait_send(13, d_r.at[1, most_r])
    exchange(3, gathered(2, True), False)
    applied = own_image(1)
    wait_send(5, rs_buf.at[1, most_r])
    wait_send(8, small.at[2, most_c])
    (curvature,) = unpack(gathered(3, False), 1)
    step_two = norm_next / curvature
    out[:PROBES, :] = step_one * d0 + step_two * d1_bf.astype(F32)
    out[PROBES:, :] = r1_own - step_two * applied
    wait_send(9, small.at[3, most_r])


def solution(mesh):
    nrow, ncol = mesh.shape["row"], mesh.shape["col"]
    xs, ys = ncol // CORES, nrow // ZS
    ngc, ngr = ZS * CORES, xs * ys

    def body(points, inv_lengths, signal_level, noise_level, right_sides, block_counts):
        vmem, smem = pl.BlockSpec(memory_space=pltpu.VMEM), pl.BlockSpec(memory_space=pltpu.SMEM)
        anywhere = pl.BlockSpec(memory_space=pl.ANY)
        result = pl.pallas_call(
            functools.partial(kernel, ngc, ngr, xs),
            out_shape=jax.ShapeDtypeStruct((2 * PROBES, BLOCK), F32),
            in_specs=[smem, smem, smem, anywhere, anywhere, anywhere],
            out_specs=vmem,
            scratch_shapes=[
                pltpu.VMEM((FEAT, BLOCK), F32),
                pltpu.VMEM((1, FEAT), F32),
                pltpu.VMEM((PROBES, BLOCK), F32),
                pltpu.SemaphoreType.DMA((3,)),
                pltpu.VMEM((FEAT, BLOCK), F32),
                pltpu.VMEM((PROBES, BLOCK), F32),
                pltpu.VMEM((2, PROBES, BLOCK), BF16),
                pltpu.VMEM((PROBES, BLOCK), F32),
                pltpu.VMEM((4, 1, 128), F32),
                pltpu.VMEM((ngc, FEAT, BLOCK), F32),
                pltpu.VMEM((ngr, FEAT, BLOCK), F32),
                pltpu.VMEM((ngc, PROBES, BLOCK), BF16),
                pltpu.VMEM((ngc, PROBES, BLOCK), F32),
                pltpu.VMEM((ngc, PROBES, BLOCK), F32),
                pltpu.VMEM((2, ngr, PROBES, BLOCK), BF16),
                pltpu.VMEM((2, ngr, PROBES, BLOCK), F32),
                pltpu.VMEM((2, ngr, PROBES, BLOCK), F32),
                pltpu.VMEM((4, ngc, 1, 128), F32),
                pltpu.VMEM((DEPTH, ngr * BLOCK), BF16),
                pltpu.VMEM((ngc * BLOCK, DEPTH), BF16),
                pltpu.VMEM((PROBES, ngc * BLOCK), BF16),
                pltpu.VMEM((ngc * BLOCK, ngr * BLOCK), BF16),
                pltpu.SemaphoreType.DMA((15,)),
                pltpu.SemaphoreType.DMA((14,)),
                pltpu.SemaphoreType.DMA((4,)),
                pltpu.SemaphoreType.DMA((ngc,)),
                pltpu.SemaphoreType.DMA((ngc,)),
                pltpu.SemaphoreType.DMA((ngc,)),
                pltpu.SemaphoreType.DMA((ngc,)),
            ],
            compiler_params=pltpu.CompilerParams(
                collective_id=0, has_side_effects=True, vmem_limit_bytes=60 * 1024 * 1024
            ),
            name="cg",
        )(block_counts, signal_level, noise_level, points.T, inv_lengths.reshape(1, FEAT), right_sides.T)
        return result[:PROBES].T, result[PROBES:].T

    in_specs = (P(("row", "col"), None), P(), P(), P(), P(("row", "col"), None), P(("row", "col")))
    out_specs = (P(("row", "col"), None), P(("row", "col"), None))
    return jax.shard_map(body, mesh=mesh, in_specs=in_specs, out_specs=out_specs, check_vma=False)
```

time: 685 us -> 75 us (0.11)
  blocking collectives: 351 us -> 0 us
  matrix products: 218 us -> 0 us
  waiting for transfers between devices: 85.9 us -> 0 us
  Pallas kernels: 0 us -> 70.7 us
  between operations: 15.4 us -> 2.58 us
    psum x3 -> x0, blocking collectives: 230 us -> none  [the longest x2 151 us: column_norm(): return lax.psum(jnp.sum(residual * residual, axis=0), ('row', 'col'))]
    dot_general x64 -> x0, matrix products: 218 us -> none  [the longest x32 166 us: kernel_tile(): lax.dot_general(scaled_rows, scaled_cols, (((1,), (1,)), ((), ())), preci...]
    all_gather x4 -> x0, blocking collectives: 121 us -> none  [the longest x2 65.7 us: column_sweep(): piece = lax.all_gather(direction, 'row', axis=0, tiled=True)]
    reduce_scatter x2 -> x0, waiting for transfers between devices: 85.9 us -> none  [body(): reduced = lax.psum_scatter(forward, 'col', scatter_dimension=0, tiled=True)]
    pallas_call x0 -> x1, Pallas kernels: none -> 70.7 us  [body(): pl.pallas_call(functools.partial(kernel, ngc, ngr, xs), out_shape=jax.Sha...]
  transfers between devices with their start and end apart: 2 -> 0, of which waited for: 2 -> 0; matrix products, arithmetic and copies ran while one was open for 0% -> 0% of each run, Pallas kernels for 0% -> 0%
where the time goes in v2:
time: 75 us; the launch traced here: 74.7 us
  Pallas kernels  70.7 us (94%)
  between operations  2.58 us (3%)
  local copies, waits for them, and re-layouts  1.4 us (2%)
    pallas_call x1, Pallas kernels, body(): pl.pallas_call(functools.partial(kernel, ngc, ngr, xs), out_shape=jax.Sha...  70.7 us

profile of v2, /device:TPU:1, one launch (start us, length us, event | category | flops | bytes accessed | tf_op | source)
XLA Modules:
  0.0 74.7 jit_solution(4565381566582432416)
XLA Ops:
  2.6 70.7 %cg.1 = f32[64,256]{1,0:T(8,128)} custom-call(s32[1]{0:T(128)S(6)} %copy.10.count, f32[1]{0:T(128)S(6)} %copy.8.signal, f32[1]{0:T(128)S(6)} %copy.9.noise, f32[16,256]{1,0:T(8,128)} %bitcast.8, f32[1,16]{1,0:T(1,128)} %bitcast.9, f32[32,256]{1,0:T(8,128)} %bitcast.7), custom_call_target="tpu_custom_call" | custom-call | tf_op jit(solution)/shard_map/cg/pallas_call | solution.py:377
  73.3 1.4 %slice_bitcast_fusion = (f32[256,32]{0,1:T(8,128)}, f32[256,32]{0,1:T(8,128)}) fusion(f32[64,256]{1,0:T(8,128)} %cg.1), kind=kLoop, calls=%fused_computation | loop fusion | bytes 131072 | tf_op jit(solution)/shard_map/transpose | solution.py:418

commit v3 on v2

v3 whole, which is shorter than its diff:
```python
import functools

import jax
import jax.numpy as jnp
from jax import lax
from jax.experimental import pallas as pl
from jax.experimental.pallas import tpu as pltpu
from jax.sharding import PartitionSpec as P

MESH = pl.DeviceIdType.MESH
F32, BF16 = jnp.float32, jnp.bfloat16
LOG2E = 1.4426950408889634

FEAT, PROBES, BLOCK = 16, 32, 256
ZS, CORES = 8, 2
DEPTH = 128


def split3(v):
    high = v.astype(BF16).astype(F32)
    rest = v - high
    mid = rest.astype(BF16).astype(F32)
    return high, mid, rest - mid


def features(points, extra, left):
    squares = jnp.sum(points * points, axis=0, keepdims=True)
    uh, um, ul = split3(extra - 0.5 * LOG2E * squares)
    row = lax.broadcasted_iota(jnp.int32, points.shape, 0)
    base, other = (0, 3) if left else (3, 0)
    tail = jnp.where(row == base, uh, jnp.where(row == base + 1, um, jnp.where(row == base + 2, ul, 0.0)))
    tail = jnp.where((row >= other) & (row < other + 3), 1.0, tail)
    h, m, l = split3(points * LOG2E if left else points)
    parts = [h, h, m, h, l, m] if left else [h, m, h, l, h, m]
    return jnp.concatenate(parts + [tail, jnp.zeros_like(points)], axis=0)


def pack(columns):
    rest = [jnp.zeros((PROBES, 1), F32)] * (128 // PROBES - len(columns))
    column = jnp.concatenate(list(columns) + rest, axis=0)
    return jnp.broadcast_to(column, (128, 128)).T[0:1, :]


def unpack(row, count):
    column = jnp.broadcast_to(row, (128, 128)).T[:, 0:1]
    return [column[i * PROBES : (i + 1) * PROBES] for i in range(count)]


def kernel(
    ngc, ngr, xs,
    count, signal, noise, points_hbm, inv_hbm, rhs_hbm,
    out,
    points, inv, rhs, load, pts_own, r0_own, d0_own, d1_own, app_own, tiles,
    pts_c, pts_r, d0_c, r0_c, app_c, d1_r, ybuf, rs_buf, small,
    amat, bmat, dmat, kmat,
    send, recv, relay, pts_sem, left_sem, d0_sem, r0_sem, ag_sem,
):
    row, col = lax.axis_index("row"), lax.axis_index("col")
    y, z = lax.div(row, ZS), lax.rem(row, ZS)
    x, core = lax.div(col, CORES), lax.rem(col, CORES)
    gc = z * CORES + core
    gr = y * xs + x
    me = (row, col)
    partner = (row, x * CORES + 1 - core)
    pairs = ngr // 2
    half = ngc * BLOCK // 2

    def around(g, k, total):
        return lax.rem(g + k, total)

    def dev_c(g):
        return (y * ZS + lax.div(g, CORES), x * CORES + lax.rem(g, CORES))

    def dev_r(g):
        return (lax.div(g, xs) * ZS + z, lax.rem(g, xs) * CORES + core)

    def at_z(dz, c=core):
        return around(z, dz % ZS, ZS) * CORES + c

    def chip_z(dz):
        return (y * ZS + around(z, dz % ZS, ZS), col)

    def pair_at(k):
        return around(lax.div(gr, 2), k, pairs)

    peers_c = [dev_c(around(gc, k, ngc)) for k in range(1, ngc)]
    peers_r = [dev_r(2 * lax.div(gr, 2) + 1 - lax.rem(gr, 2))]
    for k in range(1, pairs):
        peers_r += [dev_r(2 * pair_at(pairs - k) + h) for h in range(2)]
    first_hops, later_hops = [1, -1, 2], [-2, 3, -3, 4]
    hops = first_hops + later_hops
    places = [(dz, side) for dz in [0] + hops for side in range(2)]
    order = [at_z(-dz, 1 - core if side else core) for dz, side in places]
    others = order[1::2]
    far_source = around(z, 6 - 4 * core, ZS) * CORES + core
    far_target = (y * ZS + around(z, 2 + 4 * core, ZS), col)

    def copy(src, dst, ss, rs, dev):
        return pltpu.make_async_remote_copy(
            src_ref=src, dst_ref=dst, send_sem=ss, recv_sem=rs, device_id=dev, device_id_type=MESH
        )

    def wait_recv(i, dst):
        copy(dst, dst, send.at[i], recv.at[i], me).wait_recv()

    def wait_send(i, src):
        copy(src, src, send.at[i], recv.at[0], me).wait_send()

    most_c, most_r = pl.ds(0, ngc - 1), pl.ds(0, ngr - 1)

    def spread(i, block, slots, sems, targets):
        copy(block, slots.at[gc], send.at[i], sems.at[gc], partner).start()
        for dz in targets:
            copy(block, slots.at[gc], send.at[i], sems.at[gc], chip_z(dz)).start()

    def arrived(slots, sems, g):
        copy(slots.at[g], slots.at[g], send.at[0], sems.at[g], me).wait_recv()

    def hand_on(j, slots, sems, g, dev):
        copy(slots.at[g], slots.at[g], relay.at[j], sems.at[g], dev).start()

    def pass_over(j, slots, sems, distances):
        for dz in distances:
            arrived(slots, sems, at_z(-dz))
            hand_on(j, slots, sems, at_z(-dz), partner)

    def drain(i, j, slots, sent, handed):
        copy(slots.at[pl.ds(0, sent)], slots.at[pl.ds(0, sent)], send.at[i], recv.at[0], me).wait_send()
        copy(slots.at[pl.ds(0, handed)], slots.at[pl.ds(0, handed)], relay.at[j], recv.at[0], me).wait_send()

    loads = [
        pltpu.make_async_copy(source, target, load.at[i])
        for i, (source, target) in enumerate([(points_hbm, points), (inv_hbm, inv), (rhs_hbm, rhs)])
    ]
    for one in loads:
        one.start()
    barrier = pltpu.get_barrier_semaphore()
    for peer in peers_c + peers_r:
        pl.semaphore_signal(barrier, inc=1, device_id=peer, device_id_type=MESH)

    for one in loads:
        one.wait()
    inv_row = jnp.concatenate([inv[...], jnp.zeros((1, 128 - FEAT), F32)], axis=1)
    inv_column = jnp.broadcast_to(inv_row, (128, 128)).T[:FEAT, 0:1]
    own = points[...] * inv_column
    slot = lax.broadcasted_iota(jnp.int32, (1, BLOCK), 1)
    valid = (slot < count[0]).astype(F32)
    first = valid * rhs[...]
    first_bf = first.astype(BF16)
    d0 = first_bf.astype(F32)
    pts_own[...] = own
    pts_c[gc] = own
    pts_r[gr] = own
    r0_own[...] = first
    r0_c[gc] = first
    d0_own[...] = first_bf
    d0_c[gc] = first_bf
    pl.semaphore_wait(barrier, (ngc - 1) + (ngr - 1))

    spread(1, pts_own, pts_c, pts_sem, hops)
    for peer in peers_r:
        copy(pts_own, pts_r.at[gr], send.at[0], left_sem.at[gr], peer).start()
    spread(2, d0_own, d0_c, d0_sem, hops)
    spread(3, r0_own, r0_c, r0_sem, hops)

    log_signal = jnp.log(jnp.full((1, BLOCK), signal[0], F32)) * LOG2E

    def lanes_of(g, width=1):
        return pl.ds(pl.multiple_of(g * width * BLOCK, width * BLOCK), width * BLOCK)

    def right_block(i):
        right = features(pts_c[order[i]], jnp.zeros((1, BLOCK), F32), False).T.astype(BF16)
        bmat[i * BLOCK : (i + 1) * BLOCK, :] = right

    def left_block(g):
        amat[:, lanes_of(g)] = features(pts_r[g], log_signal, True).astype(BF16)

    right_block(0)
    left_block(gr)
    pass_over(0, pts_c, pts_sem, first_hops)
    for i in range(2, ngc // 2, 2):
        right_block(i)
    for i in range(1, ngc // 2, 2):
        arrived(pts_c, pts_sem, order[i])
        right_block(i)
    pass_over(0, pts_c, pts_sem, later_hops)

    def build(start, lanes):
        exponent = jnp.dot(bmat[start : start + half, :], amat[:, lanes], preferred_element_type=F32)
        values = jnp.exp2(exponent).astype(BF16)
        kmat[start : start + half, lanes] = values
        return values

    def near_part(k, _):
        j = pair_at(k)
        for h in range(2):

            @pl.when(2 * j + h != gr)
            def _():
                arrived(pts_r, left_sem, 2 * j + h)
                left_block(2 * j + h)

        build(0, lanes_of(j, 2))
        return 0

    lax.fori_loop(0, pairs - 3, near_part, 0)
    pass_over(1, d0_c, d0_sem, hops)
    lax.fori_loop(pairs - 3, pairs, near_part, 0)
    for i in range(ngc // 2, ngc, 2):
        right_block(i)
    for i in range(ngc // 2 + 1, ngc, 2):
        arrived(pts_c, pts_sem, order[i])
        right_block(i)
    for g in others:
        arrived(d0_c, d0_sem, g)
    for i, g in enumerate(order):
        dmat[:, i * BLOCK : (i + 1) * BLOCK] = d0_c[g]

    def send_image(it, j, image):
        for h in range(2):
            owner = 2 * j + h
            ybuf[it, owner] = image[:, h * BLOCK : (h + 1) * BLOCK]

            @pl.when(owner != gr)
            def _():
                copy(ybuf.at[it, owner], rs_buf.at[it, gr], send.at[4 + it], recv.at[4 + it], dev_r(owner)).start()

    def far_part(k, _):
        j = pair_at(k)
        lanes = lanes_of(j, 2)
        image = jnp.dot(dmat[:, :half], kmat[:half, lanes], preferred_element_type=F32)
        image = image + jnp.dot(dmat[:, half:], build(half, lanes), preferred_element_type=F32)
        send_image(0, j, image)
        return 0

    lax.fori_loop(1, pairs + 1, far_part, 0)
    pass_over(2, r0_c, r0_sem, hops)

    def sum_of(v):
        return jnp.sum(v, axis=1, keepdims=True)

    def own_image(it, direction):
        wait_recv(4 + it, rs_buf.at[it, most_r])
        rs_buf[it, gr] = ybuf[it, gr]
        return valid * jnp.sum(rs_buf[it], axis=0) + noise[0] * direction

    def exchange(s, message, along_c):
        i = 6 + s
        group, devices = (gc, peers_c) if along_c else (gr, peers_r)
        tiles[s] = message
        small[s, group] = message
        for device in devices:
            copy(tiles.at[s], small.at[s, group], send.at[i], recv.at[i], device).start()

    def gathered(s, along_c):
        wait_recv(6 + s, small.at[s, most_c if along_c else most_r])
        return small[s]

    def lane_roll(v, shift):
        return pltpu.roll(v, shift % 128, v.ndim - 1)

    def joined(part):
        weight, vertex, least = [lane_roll(part, -PROBES * i) for i in (1, 2, 3)]
        weights = jnp.sum(weight, axis=0)
        middle = jnp.where(weights > 0.0, jnp.sum(weight * vertex, axis=0) / weights, 0.0)
        away = vertex - middle[None]
        return jnp.sum(part, axis=0), weights, middle, jnp.sum(least + weight * away * away, axis=0)

    lane = lax.broadcasted_iota(jnp.int32, (1, 128), 1)

    def side_by_side(rows):
        result = rows[0]
        for i, one in enumerate(rows[1:], 1):
            result = jnp.where(lane >= PROBES * i, lane_roll(one, PROBES * i), result)
        return result

    applied = own_image(0, d0)
    app_own[...] = applied
    app_c[gc] = applied
    spread(11, app_own, app_c, ag_sem, (1, -1, 2, -2))
    weight = sum_of(applied * applied)
    vertex = jnp.where(weight > 0.0, sum_of(first * applied) / weight, 0.0)
    off = first - vertex * applied
    exchange(0, pack([sum_of(d0 * applied), weight, vertex, sum_of(off * off)]), False)
    for dz in (1, -1, 2, -2):
        g = at_z(-dz)
        arrived(app_c, ag_sem, g)
        if dz == 2 or dz == -2:
            hand_on(3, app_c, ag_sem, g, chip_z(dz // 2))
        if dz == -2:
            hand_on(3, app_c, ag_sem, far_source, far_target)
        hand_on(3, app_c, ag_sem, g, partner)
    exchange(1, side_by_side(joined(gathered(0, False))), True)
    pass_over(3, app_c, ag_sem, (3, -3, 4))
    curvature, weight, vertex, least = joined(gathered(1, True))
    norm_now = least + weight * vertex * vertex
    step_row = norm_now / curvature
    norm_next = least + weight * (step_row - vertex) * (step_row - vertex)
    step_one, beta, norm_next = unpack(side_by_side([step_row, norm_next / norm_now, norm_next]), 3)
    for g in others:
        arrived(r0_c, r0_sem, g)
    for g in others:
        arrived(app_c, ag_sem, g)
    for i, g in enumerate(order):
        r1 = r0_c[g] - step_one * app_c[g]
        dmat[:, i * BLOCK : (i + 1) * BLOCK] = (r1 + beta * d0_c[g].astype(F32)).astype(BF16)
    r1_own = first - step_one * applied
    d1_bf = (r1_own + beta * d0).astype(BF16)
    d1 = d1_bf.astype(F32)
    d1_own[...] = d1_bf
    d1_r[gr] = d1_bf
    for peer in peers_r:
        copy(d1_own, d1_r.at[gr], send.at[10], recv.at[10], peer).start()

    def second_part(k, _):
        j = pair_at(k)
        send_image(1, j, jnp.dot(dmat[...], kmat[:, lanes_of(j, 2)], preferred_element_type=F32))
        return 0

    lax.fori_loop(1, pairs + 1, second_part, 0)
    wait_recv(10, d1_r.at[most_r])
    acc = jnp.zeros((PROBES, BLOCK), F32)
    for g in range(ngr):
        acc = acc + d1_r[g].astype(F32) * ybuf[1, g]
    exchange(2, pack([sum_of(acc) + noise[0] * sum_of(d1 * d1)]), True)
    drain(1, 0, pts_c, ZS, ZS - 1)
    drain(2, 1, d0_c, ZS, ZS - 1)
    drain(3, 2, r0_c, ZS, ZS - 1)
    drain(11, 3, app_c, 5, 10)
    wait_send(0, pts_r.at[most_r])
    wait_send(4, rs_buf.at[0, most_r])
    wait_send(6, small.at[0, most_r])
    wait_send(7, small.at[1, most_c])
    exchange(3, jnp.sum(gathered(2, True), axis=0), False)
    wait_send(8, small.at[2, most_c])
    wait_send(10, d1_r.at[most_r])
    applied = own_image(1, d1)
    wait_send(5, rs_buf.at[1, most_r])
    (curvature,) = unpack(jnp.sum(gathered(3, False), axis=0), 1)
    step_two = norm_next / curvature
    out[:PROBES, :] = step_one * d0 + step_two * d1
    out[PROBES:, :] = r1_own - step_two * applied
    wait_send(9, small.at[3, most_r])


def solution(mesh):
    nrow, ncol = mesh.shape["row"], mesh.shape["col"]
    xs, ys = ncol // CORES, nrow // ZS
    ngc, ngr = ZS * CORES, xs * ys

    def body(points, inv_lengths, signal_level, noise_level, right_sides, block_counts):
        vmem, smem = pl.BlockSpec(memory_space=pltpu.VMEM), pl.BlockSpec(memory_space=pltpu.SMEM)
        anywhere = pl.BlockSpec(memory_space=pl.ANY)
        result = pl.pallas_call(
            functools.partial(kernel, ngc, ngr, xs),
            out_shape=jax.ShapeDtypeStruct((2 * PROBES, BLOCK), F32),
            in_specs=[smem, smem, smem, anywhere, anywhere, anywhere],
            out_specs=vmem,
            scratch_shapes=[
                pltpu.VMEM((FEAT, BLOCK), F32),
                pltpu.VMEM((1, FEAT), F32),
                pltpu.VMEM((PROBES, BLOCK), F32),
                pltpu.SemaphoreType.DMA((3,)),
                pltpu.VMEM((FEAT, BLOCK), F32),
                pltpu.VMEM((PROBES, BLOCK), F32),
                pltpu.VMEM((PROBES, BLOCK), BF16),
                pltpu.VMEM((PROBES, BLOCK), BF16),
                pltpu.VMEM((PROBES, BLOCK), F32),
                pltpu.VMEM((4, 1, 128), F32),
                pltpu.VMEM((ngc, FEAT, BLOCK), F32),
                pltpu.VMEM((ngr, FEAT, BLOCK), F32),
                pltpu.VMEM((ngc, PROBES, BLOCK), BF16),
                pltpu.VMEM((ngc, PROBES, BLOCK), F32),
                pltpu.VMEM((ngc, PROBES, BLOCK), F32),
                pltpu.VMEM((ngr, PROBES, BLOCK), BF16),
                pltpu.VMEM((2, ngr, PROBES, BLOCK), F32),
                pltpu.VMEM((2, ngr, PROBES, BLOCK), F32),
                pltpu.VMEM((4, ngc, 1, 128), F32),
                pltpu.VMEM((DEPTH, ngr * BLOCK), BF16),
                pltpu.VMEM((ngc * BLOCK, DEPTH), BF16),
                pltpu.VMEM((PROBES, ngc * BLOCK), BF16),
                pltpu.VMEM((ngc * BLOCK, ngr * BLOCK), BF16),
                pltpu.SemaphoreType.DMA((12,)),
                pltpu.SemaphoreType.DMA((12,)),
                pltpu.SemaphoreType.DMA((4,)),
                pltpu.SemaphoreType.DMA((ngc,)),
                pltpu.SemaphoreType.DMA((ngr,)),
                pltpu.SemaphoreType.DMA((ngc,)),
                pltpu.SemaphoreType.DMA((ngc,)),
                pltpu.SemaphoreType.DMA((ngc,)),
            ],
            compiler_params=pltpu.CompilerParams(
                collective_id=0, has_side_effects=True, vmem_limit_bytes=60 * 1024 * 1024
            ),
            name="cg",
        )(block_counts, signal_level, noise_level, points.T, inv_lengths.reshape(1, FEAT), right_sides.T)
        return result[:PROBES].T, result[PROBES:].T

    in_specs = (P(("row", "col"), None), P(), P(), P(), P(("row", "col"), None), P(("row", "col")))
    out_specs = (P(("row", "col"), None), P(("row", "col"), None))
    return jax.shard_map(body, mesh=mesh, in_specs=in_specs, out_specs=out_specs, check_vma=False)
```

time: 75 us -> 71.7 us (0.956)
  Pallas kernels: 70.7 us -> 67.5 us
    pallas_call x1, Pallas kernels: 70.7 us -> 67.5 us  [body(): pl.pallas_call(functools.partial(kernel, ngc, ngr, xs), out_shape=jax.Sha...]
where the time goes in v3:
time: 71.7 us; the launch traced here: 71.4 us
  Pallas kernels  67.5 us (94%)
  between operations  2.58 us (4%)
  local copies, waits for them, and re-layouts  1.4 us (2%)
    pallas_call x1, Pallas kernels, body(): pl.pallas_call(functools.partial(kernel, ngc, ngr, xs), out_shape=jax.Sha...  67.5 us

profile of v3, /device:TPU:1, one launch (start us, length us, event | category | flops | bytes accessed | tf_op | source)
XLA Modules:
  0.0 71.4 jit_solution(6948912477221933421)
XLA Ops:
  2.6 67.5 %cg.1 = f32[64,256]{1,0:T(8,128)} custom-call(s32[1]{0:T(128)S(6)} %copy.10.count, f32[1]{0:T(128)S(6)} %copy.8.signal, f32[1]{0:T(128)S(6)} %copy.9.noise, f32[16,256]{1,0:T(8,128)} %bitcast.8, f32[1,16]{1,0:T(1,128)} %bitcast.9, f32[32,256]{1,0:T(8,128)} %bitcast.7), custom_call_target="tpu_custom_call" | custom-call | tf_op jit(solution)/shard_map/cg/pallas_call | solution.py:354
  70.0 1.4 %slice_bitcast_fusion = (f32[256,32]{0,1:T(8,128)}, f32[256,32]{0,1:T(8,128)}) fusion(f32[64,256]{1,0:T(8,128)} %cg.1), kind=kLoop, calls=%fused_computation | loop fusion | bytes 131072 | tf_op jit(solution)/shard_map/transpose | solution.py:397

commit v4 on v3

--- a/solution.py
+++ b/solution.py
@@ -92,8 +92,6 @@
     places = [(dz, side) for dz in [0] + hops for side in range(2)]
     order = [at_z(-dz, 1 - core if side else core) for dz, side in places]
     others = order[1::2]
-    far_source = around(z, 6 - 4 * core, ZS) * CORES + core
-    far_target = (y * ZS + around(z, 2 + 4 * core, ZS), col)
 
     def copy(src, dst, ss, rs, dev):
         return pltpu.make_async_remote_copy(
@@ -192,20 +190,21 @@
         return values
 
     def near_part(k, _):
-        j = pair_at(k)
-        for h in range(2):
-
-            @pl.when(2 * j + h != gr)
+        quad = around(lax.div(gr, 4), k, quads)
+        for h in range(4):
+
+            @pl.when(4 * quad + h != gr)
             def _():
-                arrived(pts_r, left_sem, 2 * j + h)
-                left_block(2 * j + h)
-
-        build(0, lanes_of(j, 2))
+                arrived(pts_r, left_sem, 4 * quad + h)
+                left_block(4 * quad + h)
+
+        build(0, lanes_of(quad, 4))
         return 0
 
-    lax.fori_loop(0, pairs - 3, near_part, 0)
+    quads = ngr // 4
+    lax.fori_loop(0, quads - 1, near_part, 0)
     pass_over(1, d0_c, d0_sem, hops)
-    lax.fori_loop(pairs - 3, pairs, near_part, 0)
+    near_part(quads - 1, 0)
     for i in range(ngc // 2, ngc, 2):
         right_block(i)
     for i in range(ngc // 2 + 1, ngc, 2):
@@ -225,17 +224,21 @@
             def _():
                 copy(ybuf.at[it, owner], rs_buf.at[it, gr], send.at[4 + it], recv.at[4 + it], dev_r(owner)).start()
 
+    def far_image(lanes):
+        image = jnp.dot(dmat[:, :half], kmat[:half, lanes], preferred_element_type=F32)
+        return image + jnp.dot(dmat[:, half:], build(half, lanes), preferred_element_type=F32)
+
     def far_part(k, _):
         j = pair_at(k)
-        lanes = lanes_of(j, 2)
-        image = jnp.dot(dmat[:, :half], kmat[:half, lanes], preferred_element_type=F32)
-        image = image + jnp.dot(dmat[:, half:], build(half, lanes), preferred_element_type=F32)
-        send_image(0, j, image)
+        send_image(0, j, far_image(lanes_of(j, 2)))
         return 0
 
-    lax.fori_loop(1, pairs + 1, far_part, 0)
+    lax.fori_loop(1, pairs, far_part, 0)
+    twin = 2 * lax.div(gr, 2) + 1 - lax.rem(gr, 2)
+    ybuf[0, twin] = far_image(lanes_of(twin))
+    copy(ybuf.at[0, twin], rs_buf.at[0, gr], send.at[4], recv.at[4], dev_r(twin)).start()
     pass_over(2, r0_c, r0_sem, hops)
-
+    ybuf[0, gr] = far_image(lanes_of(gr))
     def sum_of(v):
         return jnp.sum(v, axis=1, keepdims=True)
 
@@ -277,21 +280,14 @@
     applied = own_image(0, d0)
     app_own[...] = applied
     app_c[gc] = applied
-    spread(11, app_own, app_c, ag_sem, (1, -1, 2, -2))
+    spread(11, app_own, app_c, ag_sem, hops)
     weight = sum_of(applied * applied)
     vertex = jnp.where(weight > 0.0, sum_of(first * applied) / weight, 0.0)
     off = first - vertex * applied
     exchange(0, pack([sum_of(d0 * applied), weight, vertex, sum_of(off * off)]), False)
-    for dz in (1, -1, 2, -2):
-        g = at_z(-dz)
-        arrived(app_c, ag_sem, g)
-        if dz == 2 or dz == -2:
-            hand_on(3, app_c, ag_sem, g, chip_z(dz // 2))
-        if dz == -2:
-            hand_on(3, app_c, ag_sem, far_source, far_target)
-        hand_on(3, app_c, ag_sem, g, partner)
+    pass_over(3, app_c, ag_sem, first_hops)
     exchange(1, side_by_side(joined(gathered(0, False))), True)
-    pass_over(3, app_c, ag_sem, (3, -3, 4))
+    pass_over(3, app_c, ag_sem, later_hops)
     curvature, weight, vertex, least = joined(gathered(1, True))
     norm_now = least + weight * vertex * vertex
     step_row = norm_now / curvature
@@ -326,7 +322,7 @@
     drain(1, 0, pts_c, ZS, ZS - 1)
     drain(2, 1, d0_c, ZS, ZS - 1)
     drain(3, 2, r0_c, ZS, ZS - 1)
-    drain(11, 3, app_c, 5, 10)
+    drain(11, 3, app_c, ZS, ZS - 1)
     wait_send(0, pts_r.at[most_r])
     wait_send(4, rs_buf.at[0, most_r])
     wait_send(6, small.at[0, most_r])

time: 71.7 us -> 70.7 us (0.986)
  Pallas kernels: 67.5 us -> 66.4 us
    pallas_call x1, Pallas kernels: 67.5 us -> 66.4 us  [body(): pl.pallas_call(functools.partial(kernel, ngc, ngr, xs), out_shape=jax.Sha...]
where the time goes in v4:
time: 70.7 us; the launch traced here: 70.4 us
  Pallas kernels  66.4 us (94%)
  between operations  2.58 us (4%)
  local copies, waits for them, and re-layouts  1.4 us (2%)
    pallas_call x1, Pallas kernels, body(): pl.pallas_call(functools.partial(kernel, ngc, ngr, xs), out_shape=jax.Sha...  66.4 us

profile of v4, /device:TPU:1, one launch (start us, length us, event | category | flops | bytes accessed | tf_op | source)
XLA Modules:
  0.0 70.4 jit_solution(13032771038176172140)
XLA Ops:
  2.6 66.4 %cg.1 = f32[64,256]{1,0:T(8,128)} custom-call(s32[1]{0:T(128)S(6)} %copy.10.count, f32[1]{0:T(128)S(6)} %copy.8.signal, f32[1]{0:T(128)S(6)} %copy.9.noise, f32[16,256]{1,0:T(8,128)} %bitcast.8, f32[1,16]{1,0:T(1,128)} %bitcast.9, f32[32,256]{1,0:T(8,128)} %bitcast.7), custom_call_target="tpu_custom_call" | custom-call | tf_op jit(solution)/shard_map/cg/pallas_call | solution.py:350
  69.0 1.4 %slice_bitcast_fusion = (f32[256,32]{0,1:T(8,128)}, f32[256,32]{0,1:T(8,128)}) fusion(f32[64,256]{1,0:T(8,128)} %cg.1), kind=kLoop, calls=%fused_computation | loop fusion | bytes 131072 | tf_op jit(solution)/shard_map/transpose | solution.py:393

commit v5 on v4

--- a/solution.py
+++ b/solution.py
@@ -280,14 +280,13 @@
     applied = own_image(0, d0)
     app_own[...] = applied
     app_c[gc] = applied
-    spread(11, app_own, app_c, ag_sem, hops)
+    spread(11, app_own, app_c, ag_sem, (4, 3, -3, 2, -2, 1, -1))
     weight = sum_of(applied * applied)
     vertex = jnp.where(weight > 0.0, sum_of(first * applied) / weight, 0.0)
     off = first - vertex * applied
     exchange(0, pack([sum_of(d0 * applied), weight, vertex, sum_of(off * off)]), False)
-    pass_over(3, app_c, ag_sem, first_hops)
     exchange(1, side_by_side(joined(gathered(0, False))), True)
-    pass_over(3, app_c, ag_sem, later_hops)
+    pass_over(3, app_c, ag_sem, (4, 3, -3, 2, -2, 1, -1))
     curvature, weight, vertex, least = joined(gathered(1, True))
     norm_now = least + weight * vertex * vertex
     step_row = norm_now / curvature

time: 70.7 us -> 70 us (0.990)
  no operation moved by 1% of the time
where the time goes in v5:
time: 70 us; the launch traced here: 69.7 us
  Pallas kernels  65.8 us (94%)
  between operations  2.58 us (4%)
  local copies, waits for them, and re-layouts  1.4 us (2%)
    pallas_call x1, Pallas kernels, body(): pl.pallas_call(functools.partial(kernel, ngc, ngr, xs), out_shape=jax.Sha...  65.8 us
    transpose x1, local copies, waits for them, and re-layouts, body(): return (result[:PROBES].T, result[PROBES:].T)  1.4 us

profile of v5, /device:TPU:1, one launch (start us, length us, event | category | flops | bytes accessed | tf_op | source)
XLA Modules:
  0.0 69.7 jit_solution(6003925321705318712)
XLA Ops:
  2.6 65.8 %cg.1 = f32[64,256]{1,0:T(8,128)} custom-call(s32[1]{0:T(128)S(6)} %copy.10.count, f32[1]{0:T(128)S(6)} %copy.8.signal, f32[1]{0:T(128)S(6)} %copy.9.noise, f32[16,256]{1,0:T(8,128)} %bitcast.8, f32[1,16]{1,0:T(1,128)} %bitcast.9, f32[32,256]{1,0:T(8,128)} %bitcast.7), custom_call_target="tpu_custom_call" | custom-call | tf_op jit(solution)/shard_map/cg/pallas_call | solution.py:349
  68.3 1.4 %slice_bitcast_fusion = (f32[256,32]{0,1:T(8,128)}, f32[256,32]{0,1:T(8,128)}) fusion(f32[64,256]{1,0:T(8,128)} %cg.1), kind=kLoop, calls=%fused_computation | loop fusion | bytes 131072 | tf_op jit(solution)/shard_map/transpose | solution.py:392
